TPU v7x, 32 devices: a whole 2x2x4 slice. The times are simulated.
32 devices in a mesh: groups: 2 (over x), tm: 16 (over z, y, core).
Axes of the slice: x: 2, y: 2, z: 4, core: 2. Of those that a mesh axis runs over, the one named last changes fastest.
Arguments:
- signal: float32 [2, 8192], P('groups', 'tm'), parts along dimension 0, may hold values from -6 to 6
- codes: bfloat16 [2, 1024, 8192], P('groups', None, 'tm'), parts along dimension 0, may hold values from -6 to 6
- dictionary: float32 [1024, 512], P('tm'), may hold values from -6 to 6
- thresholds: float32 [1024], replicated, may hold values from 0.02 to 0.2
Outputs:
- codes_out: bfloat16 [2, 1024, 8192], P('groups', None, 'tm'), parts along dimension 0
- dictionary_out: float32 [2048, 512], P(('groups', 'tm')), parts along dimension 0
- residual_out: float32 [2, 8192], P('groups', 'tm'), parts along dimension 0
There are 2 independent parts, one for each index of `groups`. A program takes and returns all parts, laid end to end along the dimension named above; an argument that names none is the same for every part. Nothing has to cross between parts.
All inputs are finite; a program needn't handle non-finite values.
Results may differ from a plain program's by a relative error of at most 0.0072.
Values may be sent and summed in bfloat16 or wider, within the bound.
A program may use at most 64 MiB of HBM per device.

v0:
```python
import functools

import jax
import jax.numpy as jnp
from jax import lax
from jax.experimental import pallas as pl
from jax.experimental.pallas import tpu as pltpu
from jax.sharding import PartitionSpec as P

ITERS = 2
CODE_STEP = 6.0
EPSILON = 1e-06
LANES = 128
MESH = pl.DeviceIdType.MESH
BF16, F32 = jnp.bfloat16, jnp.float32


def rolled(x, shift):
    width = x.shape[1]
    shift = shift % width
    return x if shift == 0 else pltpu.roll(x, shift, 1)


def skew_total(lagged):
    lag_count, time_len = lagged.shape
    width = lag_count + time_len
    total = None
    for a in range(LANES // 8):
        part = None
        for b in range(lag_count // LANES):
            block = lagged[pl.ds(b * LANES + a * 8, 8), :]
            pieces = [block]
            if b:
                pieces.insert(0, jnp.zeros((8, b * LANES), F32))
            if width - b * LANES - time_len:
                pieces.append(jnp.zeros((8, width - b * LANES - time_len), F32))
            block = jnp.concatenate(pieces, axis=1)
            part = block if part is None else part + block
        part = rolled(part, 8 * a)
        total = part if total is None else total + part
    out = total[0:1, :]
    for r in range(1, 8):
        out = out + rolled(total, r)[r : r + 1, :]
    return out


def fill_frames(frames, extended):
    lag_count, time_len = frames.shape
    width = extended.shape[1]
    wide = jnp.broadcast_to(extended, (8, width))
    row = lax.broadcasted_iota(jnp.int32, (8, width), 0)
    base = wide
    for r in range(1, 8):
        base = jnp.where(row == r, rolled(wide, width - r), base)
    for a in range(LANES // 16):
        low, high = rolled(base, width - 16 * a), rolled(base, width - 16 * a - 8)
        both = jnp.concatenate([low, high], axis=0).astype(BF16)
        for b in range(lag_count // LANES):
            frames[pl.ds(b * LANES + a * 16, 16), :] = both[:, b * LANES : b * LANES + time_len]


def kernel(
    n, signal_ref, codes_hbm, dictionary_ref, thresholds_ref,
    codes_out_hbm, atoms_ref, residual_ref,
    codes_b, current, atoms_b, lagged, frames, grad, keep,
    over_send, part_send, over_recv, part_recv, signal_next,
    core_send, core_recv, y_send, y_recv, z_send, z_recv,
    local_sem, halo_s, halo_r, sig_s, sig_r,
    az_s, az_r, ay_s, ay_r, ac_s, ac_r,
    gc_s, gc_r, gy_s, gy_r, gz_s, gz_r,
):
    rows, lag_count = dictionary_ref.shape
    atom_count, time_len = codes_b.shape
    factor = (atom_count * lag_count) ** (-0.5)
    nz = n // 4
    me = lax.axis_index("tm")
    core, y, z = me % 2, (me // 2) % 2, me // 4

    def index_of(zz, yy, cc):
        return (zz * 2 + yy) * 2 + cc

    partner = index_of(z, y, 1 - core)
    across = index_of(z, 1 - y, core)
    following, previous = (me + 1) % n, (me + n - 1) % n

    def up(d):
        return (z + d) % nz

    def down(d):
        return (z + nz - d) % nz

    def copy_to(src, dst, send_sem, recv_sem, target):
        return pltpu.make_async_remote_copy(
            src_ref=src, dst_ref=dst, send_sem=send_sem, recv_sem=recv_sem,
            device_id={"tm": target}, device_id_type=MESH,
        )

    load = pltpu.make_async_copy(codes_hbm.at[0], codes_b, local_sem.at[0])
    load.start()

    barrier = pltpu.get_barrier_semaphore()
    for target in [partner, across, following, previous] + [index_of(up(d), y, core) for d in range(1, nz)]:
        pl.semaphore_signal(barrier, inc=1, device_id={"tm": target}, device_id_type=MESH)
    pl.semaphore_wait(barrier, 4 + nz - 1)

    sent = []

    def start(copy):
        copy.start()
        sent.append(copy)

    def block(it, index):
        return atoms_b.at[it, pl.ds(pl.multiple_of(index * rows, rows), rows), :]

    def gather(it):
        def move(index, send_sem, recv_sem, target):
            return copy_to(block(it, index), block(it, index), send_sem, recv_sem, target)

        for d in range(1, nz):
            start(move(me, az_s.at[it, d], az_r.at[it, d], index_of(up(d), y, core)))
        start(move(me, ay_s.at[it, 0], ay_r.at[it, 0], across))
        start(move(me, ac_s.at[it, 0, 0], ac_r.at[it, 0, 0], partner))
        for d in range(1, nz):
            held = index_of(down(d), y, core)
            move(held, az_s.at[it, d], az_r.at[it, d], me).wait_recv()
            start(move(held, ay_s.at[it, d], ay_r.at[it, d], across))
            start(move(held, ac_s.at[it, d, 0], ac_r.at[it, d, 0], partner))
        for d in range(nz):
            held = index_of(down(d), 1 - y, core)
            move(held, ay_s.at[it, d], ay_r.at[it, d], across).wait_recv()
            start(move(held, ac_s.at[it, d, 1], ac_r.at[it, d, 1], partner))
        for d in range(nz):
            for e in range(2):
                held = index_of(down(d), y if e == 0 else 1 - y, 1 - core)
                move(held, ac_s.at[it, d, e], ac_r.at[it, d, e], partner).wait_recv()

    atoms_ref[...] = dictionary_ref[...]
    block(0, me)[...] = dictionary_ref[...].astype(BF16)
    signal_copy = copy_to(signal_ref, signal_next, sig_s, sig_r, previous)

    @pl.when(me > 0)
    def _():
        signal_copy.start()

    for it in range(ITERS):
        last = it == ITERS - 1
        gather(it)
        if it == 0:
            load.wait()
        lagged[...] = lax.dot_general(
            atoms_b[it], codes_b[...], (((0,), (0,)), ((), ())), preferred_element_type=F32
        )
        summed = skew_total(lagged)
        mine, over = summed[:, :time_len], summed[:, time_len:]
        over_send[it] = over
        part_send[it] = mine
        over_copy = copy_to(over_send.at[it], over_recv.at[it], halo_s.at[it, 0], halo_r.at[it, 0], following)
        part_copy = copy_to(part_send.at[it], part_recv.at[it], halo_s.at[it, 1], halo_r.at[it, 1], previous)

        @pl.when(me < n - 1)
        def _():
            over_copy.start()

        @pl.when(me > 0)
        def _():
            part_copy.start()

        @pl.when(me > 0)
        def _():
            over_copy.wait_recv()

        @pl.when(me == 0)
        def _():
            over_recv[it] = jnp.zeros_like(over)

        @pl.when(me < n - 1)
        def _():
            part_copy.wait_recv()
            if it == 0:
                signal_copy.wait_recv()

        @pl.when(me == n - 1)
        def _():
            part_recv[it] = -over
            if it == 0:
                signal_next[...] = jnp.zeros_like(over)

        residual = signal_ref[...] - factor * (mine + over_recv[it])
        ahead = signal_next[...] - factor * (part_recv[it] + over)
        if last:
            residual_ref[...] = residual
        extended = jnp.concatenate([residual, ahead], axis=1).astype(BF16).astype(F32)
        fill_frames(frames, extended)

        order = list(range(1, nz)) + [0]
        layer = 4 * rows

        def own(d, yy, cc):
            return grad[d, pl.ds(pl.multiple_of((yy * 2 + cc) * rows, rows), rows), :]

        core_copies, y_copies, z_copies = {}, {}, {}
        for d in order:
            picked = pl.ds(pl.multiple_of(up(d) * layer, layer), layer)
            grad[d] = jnp.dot(codes_b[picked, :], frames[...], preferred_element_type=F32)
            core_send[it, d, 0] = own(d, y, 1 - core).astype(BF16)
            core_send[it, d, 1] = own(d, 1 - y, 1 - core).astype(BF16)
            core_copies[d] = copy_to(
                core_send.at[it, d], core_recv.at[it, d], gc_s.at[it, d], gc_r.at[it, d], partner
            )
            start(core_copies[d])
        for d in order:
            core_copies[d].wait_recv()
            y_send[it, d] = (own(d, 1 - y, core) + core_recv[it, d, 1].astype(F32)).astype(BF16)
            keep[d] = own(d, y, core) + core_recv[it, d, 0].astype(F32)
            y_copies[d] = copy_to(y_send.at[it, d], y_recv.at[it, d], gy_s.at[it, d], gy_r.at[it, d], across)
            start(y_copies[d])

        step_rows = min(256, atom_count)

        def advance(i, carry):
            picked = pl.ds(pl.multiple_of(i * step_rows, step_rows), step_rows)
            matched = jnp.dot(atoms_b[it, picked, :], frames[...], preferred_element_type=F32)
            before = codes_b[picked, :].astype(F32) if it == 0 else current[picked, :]
            shrink = before + (CODE_STEP * factor) * matched
            cutoff = CODE_STEP * thresholds_ref[picked, :]
            after = shrink - jnp.minimum(jnp.maximum(shrink, -cutoff), cutoff)
            if not last:
                current[picked, :] = after
            codes_b[picked, :] = after.astype(BF16)
            return carry

        lax.fori_loop(0, atom_count // step_rows, advance, 0)
        if last:
            store = pltpu.make_async_copy(codes_b, codes_out_hbm.at[0], local_sem.at[1])
            store.start()

        for d in order:
            y_copies[d].wait_recv()
            keep[d] = keep[d] + y_recv[it, d].astype(F32)
            if d:
                z_send[it, d] = keep[d].astype(BF16)
                z_copies[d] = copy_to(
                    z_send.at[it, d], z_recv.at[it, d], gz_s.at[it, d], gz_r.at[it, d], index_of(up(d), y, core)
                )
                start(z_copies[d])
        total = keep[0]
        for d in range(1, nz):
            z_copies[d].wait_recv()
            total = total + z_recv[it, d].astype(F32)
        updated = atoms_ref[...] + factor * total
        fresh = updated / jnp.sqrt(jnp.mean(updated * updated, axis=1, keepdims=True) + EPSILON)
        atoms_ref[...] = fresh
        if not last:
            block(it + 1, me)[...] = fresh.astype(BF16)

        @pl.when(me < n - 1)
        def _():
            over_copy.wait_send()

        @pl.when(me > 0)
        def _():
            part_copy.wait_send()

    @pl.when(me > 0)
    def _():
        signal_copy.wait_send()

    for copy in sent:
        copy.wait_send()
    store.wait()


def on_device(n, signal, codes, dictionary, thresholds):
    _, atom_count, time_len = codes.shape
    rows, lag_count = dictionary.shape
    nz = n // 4
    vmem, dma = pltpu.VMEM, pltpu.SemaphoreType.DMA
    inside = pl.BlockSpec(memory_space=pltpu.VMEM)
    outside = pl.BlockSpec(memory_space=pl.ANY)
    piece = (rows, lag_count)
    return tuple(
        pl.pallas_call(
            functools.partial(kernel, n),
            name="learn",
            out_shape=(
                jax.ShapeDtypeStruct(codes.shape, BF16),
                jax.ShapeDtypeStruct(piece, F32),
                jax.ShapeDtypeStruct(signal.shape, F32),
            ),
            in_specs=[inside, outside, inside, inside],
            out_specs=(outside, inside, inside),
            scratch_shapes=[
                vmem((atom_count, time_len), BF16),
                vmem((atom_count, time_len), F32),
                vmem((ITERS, atom_count, lag_count), BF16),
                vmem((lag_count, time_len), F32),
                vmem((lag_count, time_len), BF16),
                vmem((nz, 4 * rows, lag_count), F32),
                vmem((nz, *piece), F32),
                vmem((ITERS, 1, time_len), F32),
                vmem((ITERS, 1, time_len), F32),
                vmem((ITERS, 1, time_len), F32),
                vmem((ITERS, 1, time_len), F32),
                vmem((1, time_len), F32),
                vmem((ITERS, nz, 2, *piece), BF16),
                vmem((ITERS, nz, 2, *piece), BF16),
                vmem((ITERS, nz, *piece), BF16),
                vmem((ITERS, nz, *piece), BF16),
                vmem((ITERS, nz, *piece), BF16),
                vmem((ITERS, nz, *piece), BF16),
                dma((2,)),
                dma((ITERS, 2)),
                dma((ITERS, 2)),
                dma,
                dma,
                *[dma((ITERS, nz))] * 4,
                *[dma((ITERS, nz, 2))] * 2,
                *[dma((ITERS, nz))] * 6,
            ],
            compiler_params=pltpu.CompilerParams(
                collective_id=0, has_side_effects=True, vmem_limit_bytes=48 * 1024 * 1024
            ),
        )(signal, codes, dictionary, thresholds[:, None])
    )


def solution(mesh):
    return jax.shard_map(
        functools.partial(on_device, mesh.shape["tm"]),
        mesh=mesh,
        in_specs=(P("groups", "tm"), P("groups", None, "tm"), P("tm", None), P()),
        out_specs=(P("groups", None, "tm"), P(("groups", "tm"), None), P("groups", "tm")),
        check_vma=False,
    )
```

profile of v0, /device:TPU:0, one launch (start us, length us, event | category | flops | bytes accessed | tf_op | source)
XLA Modules:
  0.0 68.5 jit_solution(15284531229902587235)
XLA Ops:
  0.6 0.0 copy-start.1
  0.6 0.0 copy-start.2
  0.7 0.9 %copy.7.thresholds_ref = f32[1024,1]{1,0:T(8,128)S(1)} copy(f32[1024,1]{0,1:T(1,128)} %bitcast.1) | data formatting | bytes 8192 | tf_op jit(solution)/shard_map/broadcast_in_dim | solution.py:323
  1.6 0.0 copy-done.1
  1.6 0.0 copy-done.2
  1.6 0.0 copy-start
  1.6 1.2 %copy-done = bf16[1,1024,512]{2,1,0:T(8,128)(2,1)S(1)} copy-done((bf16[1,1024,512]{2,1,0:T(8,128)(2,1)S(1)}, bf16[1,1024,512]{2,1,0:T(8,128)(2,1)}, u32[]{:S(2)}) %copy-start) | copy-done | bytes 1048600
  2.8 63.5 %learn.1 = (bf16[1,1024,512]{2,1,0:T(8,128)(2,1)S(1)}, f32[64,512]{1,0:T(8,128)S(1)}, f32[1,512]{1,0:T(1,128)S(1)}) custom-call(f32[1,512]{1,0:T(1,128)S(1)} %copy-done.2, bf16[1,1024,512]{2,1,0:T(8,128)(2,1)S(1)} %copy-done, f32[64,512]{1,0:T(8,128)S(1)} %copy-done.1, f32[1024,1]{1,0:T(8,128)S(1)} %copy.7.thresholds_ref), custom_call_target="tpu_custom_call" | custom-call | tf_op jit(solution)/shard_map/learn/pallas_call | solution.py:282
  66.3 1.0 %copy.11 = bf16[1,1024,512]{2,1,0:T(8,128)(2,1)} copy(bf16[1,1024,512]{2,1,0:T(8,128)(2,1)S(1)} %get-tuple-element.6) | data formatting | bytes 2097152
  67.3 0.7 copy.12
  68.0 0.6 copy.13
Async XLA Ops:
  0.6 1.0 %copy-start.1 = (f32[64,512]{1,0:T(8,128)S(1)}, f32[64,512]{1,0:T(8,128)}, u32[]{:S(2)}) copy-start(f32[64,512]{1,0:T(8,128)} %dictionary_ref.1) | copy-start | bytes 393220
  0.6 1.0 %copy-start.2 = (f32[1,512]{1,0:T(1,128)S(1)}, f32[1,512]{1,0:T(1,128)}, u32[]{:S(2)}) copy-start(f32[1,512]{1,0:T(1,128)} %signal_ref.1) | copy-start | bytes 6148
  1.6 1.2 %copy-start = (bf16[1,1024,512]{2,1,0:T(8,128)(2,1)S(1)}, bf16[1,1024,512]{2,1,0:T(8,128)(2,1)}, u32[]{:S(2)}) copy-start(bf16[1,1024,512]{2,1,0:T(8,128)(2,1)} %codes_hbm.1) | copy-start | bytes 3145732
where the time goes:
time: 68.7 us; the launch traced here: 68.5 us
  Pallas kernels  63.5 us (92%)
  local copies, waits for them, and re-layouts  4.37 us (6%)
  between operations  0.69 us (1%)
    pallas_call x1, Pallas kernels, on_device(): pl.pallas_call(functools.partial(kernel, n), name='learn', out_shape=(jax...  63.5 us
    unnamed x9, local copies, waits for them, and re-layouts  3.43 us

commit v1 on v0

--- a/solution.py
+++ b/solution.py
@@ -13,6 +13,13 @@
 LANES = 128
 MESH = pl.DeviceIdType.MESH
 BF16, F32 = jnp.bfloat16, jnp.float32
+
+
+PIECES = 2
+
+
+def pieces_of(rows):
+    return max(1, min(PIECES, rows // 16))
 
 
 def rolled(x, shift):
@@ -60,9 +67,9 @@
 
 
 def kernel(
-    n, signal_ref, codes_hbm, dictionary_ref, thresholds_ref,
+    n, signal_hbm, codes_hbm, dictionary_hbm, thresholds_hbm,
     codes_out_hbm, atoms_ref, residual_ref,
-    codes_b, current, atoms_b, lagged, frames, grad, keep,
+    signal_ref, dictionary_ref, thresholds_ref, cutoffs, codes_b, current, atoms_b, lagged, frames, grad, keep,
     over_send, part_send, over_recv, part_recv, signal_next,
     core_send, core_recv, y_send, y_recv, z_send, z_recv,
     local_sem, halo_s, halo_r, sig_s, sig_r,
@@ -83,11 +90,19 @@
     across = index_of(z, 1 - y, core)
     following, previous = (me + 1) % n, (me + n - 1) % n
 
-    def up(d):
-        return (z + d) % nz
-
-    def down(d):
-        return (z + nz - d) % nz
+    upper = (z * 2) // nz
+
+    def layer_at(d):
+        if d == nz - 1:
+            return z
+        fall, rise = nz - 1 - d, d
+        fall = fall - (z - fall + nz) // nz
+        rise = rise + (rise - z + nz) // nz
+        return upper * rise + (1 - upper) * fall
+
+    layers = [layer_at(d) for d in range(nz)]
+    others = range(nz - 1)
+    mine_at = nz - 1
 
     def copy_to(src, dst, send_sem, recv_sem, target):
         return pltpu.make_async_remote_copy(
@@ -95,11 +110,17 @@
             device_id={"tm": target}, device_id_type=MESH,
         )
 
-    load = pltpu.make_async_copy(codes_hbm.at[0], codes_b, local_sem.at[0])
-    load.start()
+    loads = [
+        pltpu.make_async_copy(dictionary_hbm, dictionary_ref, local_sem.at[1]),
+        pltpu.make_async_copy(signal_hbm, signal_ref, local_sem.at[2]),
+        pltpu.make_async_copy(thresholds_hbm, thresholds_ref, local_sem.at[3]),
+        pltpu.make_async_copy(codes_hbm.at[0], codes_b, local_sem.at[0]),
+    ]
+    for load in loads:
+        load.start()
 
     barrier = pltpu.get_barrier_semaphore()
-    for target in [partner, across, following, previous] + [index_of(up(d), y, core) for d in range(1, nz)]:
+    for target in [partner, across, following, previous] + [index_of(layers[d], y, core) for d in others]:
         pl.semaphore_signal(barrier, inc=1, device_id={"tm": target}, device_id_type=MESH)
     pl.semaphore_wait(barrier, 4 + nz - 1)
 
@@ -112,28 +133,49 @@
     def block(it, index):
         return atoms_b.at[it, pl.ds(pl.multiple_of(index * rows, rows), rows), :]
 
+    pieces = pieces_of(rows)
+    part = rows // pieces
+
     def gather(it):
-        def move(index, send_sem, recv_sem, target):
-            return copy_to(block(it, index), block(it, index), send_sem, recv_sem, target)
-
-        for d in range(1, nz):
-            start(move(me, az_s.at[it, d], az_r.at[it, d], index_of(up(d), y, core)))
-        start(move(me, ay_s.at[it, 0], ay_r.at[it, 0], across))
-        start(move(me, ac_s.at[it, 0, 0], ac_r.at[it, 0, 0], partner))
-        for d in range(1, nz):
-            held = index_of(down(d), y, core)
-            move(held, az_s.at[it, d], az_r.at[it, d], me).wait_recv()
-            start(move(held, ay_s.at[it, d], ay_r.at[it, d], across))
-            start(move(held, ac_s.at[it, d, 0], ac_r.at[it, d, 0], partner))
-        for d in range(nz):
-            held = index_of(down(d), 1 - y, core)
-            move(held, ay_s.at[it, d], ay_r.at[it, d], across).wait_recv()
-            start(move(held, ac_s.at[it, d, 1], ac_r.at[it, d, 1], partner))
+        def move(index, q, send_sem, recv_sem, target):
+            held = atoms_b.at[it, pl.ds(pl.multiple_of(index * rows + q * part, part), part), :]
+            return copy_to(held, held, send_sem, recv_sem, target)
+
+        def to_across(index, d, q):
+            return move(index, q, ay_s.at[it, d, q], ay_r.at[it, d, q], across)
+
+        def to_partner(index, d, e, q):
+            return move(index, q, ac_s.at[it, d, e, q], ac_r.at[it, d, e, q], partner)
+
+        for q in range(pieces):
+            for d in others:
+                start(move(me, q, az_s.at[it, d, q], az_r.at[it, z, q], index_of(layers[d], y, core)))
+            start(to_across(me, mine_at, q))
+        for q in range(pieces):
+            start(to_partner(me, mine_at, 0, q))
+        for q in range(pieces):
+            for d in others:
+                held = index_of(layers[d], y, core)
+                move(held, q, az_s.at[it, d, q], az_r.at[it, layers[d], q], across).wait_recv()
+                start(to_across(held, d, q))
+                start(to_partner(held, d, 0, q))
+        for q in range(pieces):
+            held = index_of(z, 1 - y, core)
+            to_across(held, mine_at, q).wait_recv()
+            start(to_partner(held, mine_at, 1, q))
+        for q in range(pieces):
+            for d in others:
+                held = index_of(layers[d], 1 - y, core)
+                to_across(held, d, q).wait_recv()
+                start(to_partner(held, d, 1, q))
         for d in range(nz):
             for e in range(2):
-                held = index_of(down(d), y if e == 0 else 1 - y, 1 - core)
-                move(held, ac_s.at[it, d, e], ac_r.at[it, d, e], partner).wait_recv()
-
+                for q in range(pieces):
+                    held = index_of(layers[d], y if e == 0 else 1 - y, 1 - core)
+                    to_partner(held, d, e, q).wait_recv()
+
+    loads[0].wait()
+    loads[1].wait()
     atoms_ref[...] = dictionary_ref[...]
     block(0, me)[...] = dictionary_ref[...].astype(BF16)
     signal_copy = copy_to(signal_ref, signal_next, sig_s, sig_r, previous)
@@ -146,7 +188,9 @@
         last = it == ITERS - 1
         gather(it)
         if it == 0:
-            load.wait()
+            loads[2].wait()
+            cutoffs[...] = CODE_STEP * jnp.broadcast_to(thresholds_ref[...], (8, atom_count)).T[:, 0:1]
+            loads[3].wait()
         lagged[...] = lax.dot_general(
             atoms_b[it], codes_b[...], (((0,), (0,)), ((), ())), preferred_element_type=F32
         )
@@ -192,7 +236,7 @@
         extended = jnp.concatenate([residual, ahead], axis=1).astype(BF16).astype(F32)
         fill_frames(frames, extended)
 
-        order = list(range(1, nz)) + [0]
+        order = range(nz)
         layer = 4 * rows
 
         def own(d, yy, cc):
@@ -200,7 +244,7 @@
 
         core_copies, y_copies, z_copies = {}, {}, {}
         for d in order:
-            picked = pl.ds(pl.multiple_of(up(d) * layer, layer), layer)
+            picked = pl.ds(pl.multiple_of(layers[d] * layer, layer), layer)
             grad[d] = jnp.dot(codes_b[picked, :], frames[...], preferred_element_type=F32)
             core_send[it, d, 0] = own(d, y, 1 - core).astype(BF16)
             core_send[it, d, 1] = own(d, 1 - y, 1 - core).astype(BF16)
@@ -208,6 +252,21 @@
                 core_send.at[it, d], core_recv.at[it, d], gc_s.at[it, d], gc_r.at[it, d], partner
             )
             start(core_copies[d])
+        step_rows = min(256, atom_count)
+        steps = atom_count // step_rows
+
+        def advance(i):
+            picked = pl.ds(i * step_rows, step_rows)
+            matched = jnp.dot(atoms_b[it, picked, :], frames[...], preferred_element_type=F32)
+            before = codes_b[picked, :].astype(F32) if it == 0 else current[picked, :]
+            shrink = before + (CODE_STEP * factor) * matched
+            cutoff = cutoffs[picked, :]
+            after = shrink - jnp.minimum(jnp.maximum(shrink, -cutoff), cutoff)
+            if not last:
+                current[picked, :] = after
+            codes_b[picked, :] = after.astype(BF16)
+
+        advance(0)
         for d in order:
             core_copies[d].wait_recv()
             y_send[it, d] = (own(d, 1 - y, core) + core_recv[it, d, 1].astype(F32)).astype(BF16)
@@ -215,38 +274,27 @@
             y_copies[d] = copy_to(y_send.at[it, d], y_recv.at[it, d], gy_s.at[it, d], gy_r.at[it, d], across)
             start(y_copies[d])
 
-        step_rows = min(256, atom_count)
-
-        def advance(i, carry):
-            picked = pl.ds(pl.multiple_of(i * step_rows, step_rows), step_rows)
-            matched = jnp.dot(atoms_b[it, picked, :], frames[...], preferred_element_type=F32)
-            before = codes_b[picked, :].astype(F32) if it == 0 else current[picked, :]
-            shrink = before + (CODE_STEP * factor) * matched
-            cutoff = CODE_STEP * thresholds_ref[picked, :]
-            after = shrink - jnp.minimum(jnp.maximum(shrink, -cutoff), cutoff)
-            if not last:
-                current[picked, :] = after
-            codes_b[picked, :] = after.astype(BF16)
-            return carry
-
-        lax.fori_loop(0, atom_count // step_rows, advance, 0)
+        for i in range(1, steps - 1):
+            advance(i)
+        for d in order:
+            y_copies[d].wait_recv()
+            keep[d] = keep[d] + y_recv[it, d].astype(F32)
+            if d != mine_at:
+                z_send[it, d] = keep[d].astype(BF16)
+                z_copies[d] = copy_to(
+                    z_send.at[it, d], z_recv.at[it, z], gz_s.at[it, d], gz_r.at[it, z], index_of(layers[d], y, core)
+                )
+                start(z_copies[d])
+        advance(steps - 1)
         if last:
             store = pltpu.make_async_copy(codes_b, codes_out_hbm.at[0], local_sem.at[1])
             store.start()
-
-        for d in order:
-            y_copies[d].wait_recv()
-            keep[d] = keep[d] + y_recv[it, d].astype(F32)
-            if d:
-                z_send[it, d] = keep[d].astype(BF16)
-                z_copies[d] = copy_to(
-                    z_send.at[it, d], z_recv.at[it, d], gz_s.at[it, d], gz_r.at[it, d], index_of(up(d), y, core)
-                )
-                start(z_copies[d])
-        total = keep[0]
-        for d in range(1, nz):
-            z_copies[d].wait_recv()
-            total = total + z_recv[it, d].astype(F32)
+        total = keep[mine_at]
+        for d in others:
+            copy_to(
+                z_send.at[it, d], z_recv.at[it, layers[d]], gz_s.at[it, d], gz_r.at[it, layers[d]], across
+            ).wait_recv()
+            total = total + z_recv[it, layers[d]].astype(F32)
         updated = atoms_ref[...] + factor * total
         fresh = updated / jnp.sqrt(jnp.mean(updated * updated, axis=1, keepdims=True) + EPSILON)
         atoms_ref[...] = fresh
@@ -276,7 +324,7 @@
     nz = n // 4
     vmem, dma = pltpu.VMEM, pltpu.SemaphoreType.DMA
     inside = pl.BlockSpec(memory_space=pltpu.VMEM)
-    outside = pl.BlockSpec(memory_space=pl.ANY)
+    outside = pl.BlockSpec(memory_space=pltpu.HBM)
     piece = (rows, lag_count)
     return tuple(
         pl.pallas_call(
@@ -287,9 +335,13 @@
                 jax.ShapeDtypeStruct(piece, F32),
                 jax.ShapeDtypeStruct(signal.shape, F32),
             ),
-            in_specs=[inside, outside, inside, inside],
-            out_specs=(outside, inside, inside),
+            in_specs=[outside] * 4,
+            out_specs=(pl.BlockSpec(memory_space=pl.ANY), inside, inside),
             scratch_shapes=[
+                vmem(signal.shape, F32),
+                vmem(piece, F32),
+                vmem((1, atom_count), F32),
+                vmem((atom_count, 1), F32),
                 vmem((atom_count, time_len), BF16),
                 vmem((atom_count, time_len), F32),
                 vmem((ITERS, atom_count, lag_count), BF16),
@@ -308,19 +360,19 @@
                 vmem((ITERS, nz, *piece), BF16),
                 vmem((ITERS, nz, *piece), BF16),
                 vmem((ITERS, nz, *piece), BF16),
-                dma((2,)),
+                dma((4,)),
                 dma((ITERS, 2)),
                 dma((ITERS, 2)),
                 dma,
                 dma,
-                *[dma((ITERS, nz))] * 4,
-                *[dma((ITERS, nz, 2))] * 2,
+                *[dma((ITERS, nz, pieces_of(rows)))] * 4,
+                *[dma((ITERS, nz, 2, pieces_of(rows)))] * 2,
                 *[dma((ITERS, nz))] * 6,
             ],
             compiler_params=pltpu.CompilerParams(
-                collective_id=0, has_side_effects=True, vmem_limit_bytes=48 * 1024 * 1024
+                collective_id=0, has_side_effects=True, vmem_limit_bytes=66_000_000
             ),
-        )(signal, codes, dictionary, thresholds[:, None])
+        )(signal, codes, dictionary, thresholds[None, :])
     )
 
 

time: 68.7 us -> 65.4 us (0.952)
  Pallas kernels: 63.5 us -> 61 us
  local copies, waits for them, and re-layouts: 4.37 us -> 3.56 us
    pallas_call x1, Pallas kernels: 63.5 us -> 61 us  [on_device(): pl.pallas_call(functools.partial(kernel, n), name='learn', out_shape=(jax...]
    broadcast_in_dim x1 -> x0, local copies, waits for them, and re-layouts: 0.94 us -> none  [on_device(): thresholds[:, None]]
    unnamed x9 -> x7, local copies, waits for them, and re-layouts: 3.43 us -> 3.56 us
where the time goes in v1:
time: 65.4 us; the launch traced here: 65.2 us
  Pallas kernels  61 us (93%)
  local copies, waits for them, and re-layouts  3.56 us (5%)
    pallas_call x1, Pallas kernels, on_device(): pl.pallas_call(functools.partial(kernel, n), name='learn', out_shape=(jax...  61 us
    unnamed x7, local copies, waits for them, and re-layouts  3.56 us

profile of v1, /device:TPU:0, one launch (start us, length us, event | category | flops | bytes accessed | tf_op | source)
XLA Modules:
  0.0 65.2 jit_solution(4758484575713874766)
XLA Ops:
  0.6 61.0 %learn.1 = (bf16[1,1024,512]{2,1,0:T(8,128)(2,1)}, f32[64,512]{1,0:T(8,128)}, f32[1,512]{1,0:T(1,128)}) custom-call(f32[1,512]{1,0:T(1,128)} %signal_hbm.1, bf16[1,1024,512]{2,1,0:T(8,128)(2,1)} %codes_hbm.1, f32[64,512]{1,0:T(8,128)} %dictionary_hbm.1, f32[1,1024]{1,0:T(1,128)} %bitcast.1), custom_call_target="tpu_custom_call" | custom-call | tf_op jit(solution)/shard_map/learn/pallas_call | solution.py:330
  61.6 0.0 copy-start
  61.7 2.3 %copy.10 = bf16[1,1024,512]{2,1,0:T(8,128)(2,1)} copy(bf16[1,1024,512]{2,1,0:T(8,128)(2,1)} %get-tuple-element.6) | data formatting | bytes 2097152
  63.9 0.0 copy-done
  64.0 0.0 copy-start.1
  64.0 0.7 %copy.11 = f32[64,512]{1,0:T(8,128)} copy(f32[64,512]{1,0:T(8,128)S(1)} %copy-done) | data formatting | bytes 262144
  64.6 0.0 copy-done.1
  64.6 0.6 copy.12
Async XLA Ops:
  61.6 2.3 %copy-start = (f32[64,512]{1,0:T(8,128)S(1)}, f32[64,512]{1,0:T(8,128)}, u32[]{:S(2)}) copy-start(f32[64,512]{1,0:T(8,128)} %get-tuple-element.7) | copy-start | bytes 393220
  64.0 0.7 %copy-start.1 = (f32[1,512]{1,0:T(1,128)S(1)}, f32[1,512]{1,0:T(1,128)}, u32[]{:S(2)}) copy-start(f32[1,512]{1,0:T(1,128)} %get-tuple-element.8) | copy-start | bytes 6148

commit v2 on v1

--- a/solution.py
+++ b/solution.py
@@ -326,7 +326,7 @@
     inside = pl.BlockSpec(memory_space=pltpu.VMEM)
     outside = pl.BlockSpec(memory_space=pltpu.HBM)
     piece = (rows, lag_count)
-    return tuple(
+    made = tuple(
         pl.pallas_call(
             functools.partial(kernel, n),
             name="learn",
@@ -375,6 +375,33 @@
         )(signal, codes, dictionary, thresholds[None, :])
     )
 
+    quarter = atom_count // 4
+
+    def publish(codes_ref, atoms_ref, residual_ref, codes_out, atoms_out, residual_out, held, atoms, residual, sem_in, sem_out):
+        views = [
+            [ref.at[0, pl.ds(i * quarter, quarter), :] for ref in (codes_ref, held, codes_out)] for i in range(4)
+        ] + [[atoms_ref, atoms, atoms_out], [residual_ref, residual, residual_out]]
+        takes = [pltpu.make_async_copy(view[0], view[1], sem_in.at[i]) for i, view in enumerate(views)]
+        puts = [pltpu.make_async_copy(view[1], view[2], sem_out.at[i]) for i, view in enumerate(views)]
+        for take in takes:
+            take.start()
+        for take, put in zip(takes, puts):
+            take.wait()
+            put.start()
+        for put in puts:
+            put.wait()
+
+    return tuple(
+        pl.pallas_call(
+            publish,
+            name="publish",
+            out_shape=tuple(jax.ShapeDtypeStruct(x.shape, x.dtype) for x in made),
+            in_specs=[outside] * 3,
+            out_specs=(outside,) * 3,
+            scratch_shapes=[*[vmem(x.shape, x.dtype) for x in made], dma((6,)), dma((6,))],
+        )(*made)
+    )
+
 
 def solution(mesh):
     return jax.shard_map(

time: 65.4 us -> 63.8 us (0.976)
  local copies, waits for them, and re-layouts: 3.56 us -> 0 us
  Pallas kernels: 61 us -> 63.1 us
    unnamed x7 -> x0, local copies, waits for them, and re-layouts: 3.56 us -> none
    pallas_call x0 -> x1, Pallas kernels: none -> 2.06 us  [on_device(): pl.pallas_call(publish, name='publish', out_shape=tuple((jax.ShapeDtypeSt...]
where the time goes in v2:
time: 63.8 us; the launch traced here: 63.7 us
  Pallas kernels  63.1 us (99%)
  between operations  0.64 us (1%)
    pallas_call x1, Pallas kernels, on_device(): pl.pallas_call(functools.partial(kernel, n), name='learn', out_shape=(jax...  61 us
    pallas_call x1, Pallas kernels, on_device(): pl.pallas_call(publish, name='publish', out_shape=tuple((jax.ShapeDtypeSt...  2.06 us

profile of v2, /device:TPU:0, one launch (start us, length us, event | category | flops | bytes accessed | tf_op | source)
XLA Modules:
  0.0 63.7 jit_solution(16795501529163376323)
XLA Ops:
  0.6 61.0 %learn.1 = (bf16[1,1024,512]{2,1,0:T(8,128)(2,1)}, f32[64,512]{1,0:T(8,128)}, f32[1,512]{1,0:T(1,128)}) custom-call(f32[1,512]{1,0:T(1,128)} %signal_hbm.1, bf16[1,1024,512]{2,1,0:T(8,128)(2,1)} %codes_hbm.1, f32[64,512]{1,0:T(8,128)} %dictionary_hbm.1, f32[1,1024]{1,0:T(1,128)} %bitcast.1), custom_call_target="tpu_custom_call" | custom-call | tf_op jit(solution)/shard_map/learn/pallas_call | solution.py:330
  61.6 2.1 %publish.1 = (bf16[1,1024,512]{2,1,0:T(8,128)(2,1)}, f32[64,512]{1,0:T(8,128)}, f32[1,512]{1,0:T(1,128)}) custom-call(bf16[1,1024,512]{2,1,0:T(8,128)(2,1)} %get-tuple-element.6.codes_ref, f32[64,512]{1,0:T(8,128)} %get-tuple-element.7.atoms_ref, f32[1,512]{1,0:T(1,128)} %get-tuple-element.8.residual_ref), custom_call_target="tpu_custom_call" | custom-call | tf_op jit(solution)/shard_map/publish/pallas_call | solution.py:395
